TPU v7x, 128 devices: a whole 4x4x4 slice. The times are simulated.
128 devices in a mesh: dp: 8 (over y, z_hi), proto: 16 (over z_lo, x, core).
Axes of the slice: x: 4, y: 4, z: 4 (z_hi: 2, z_lo: 2; z = z_hi * 2 + z_lo), core: 2. Of those that a mesh axis runs over, the one named last changes fastest.
Arguments:
- student_patch: bfloat16 [8, 2048, 256], P('dp', 'proto'), may hold values from -4 to 4
- teacher_patch: bfloat16 [8, 2048, 256], P('dp', 'proto'), may hold values from -4 to 4
- patch_image: int32 [8, 2048], P('dp', 'proto'), may hold values from 0 to 7, never falling along the last dimension, each value on 1 to 512 neighbouring positions
- masked_rows: int32 [8, 1024], P('dp', 'proto'), may hold values from 0 to 127, as said below
- student_proto: float32 [256, 131072], P(None, 'proto'), as said below
- teacher_proto: float32 [256, 131072], P(None, 'proto'), as said below
- first_moment: float32 [256, 131072], P('dp', 'proto'), as said below
- second_moment: float32 [256, 131072], P('dp', 'proto'), as said below
- centre: float32 [131072], P('proto'), may hold values from -0.3 to 0.3
Outputs:
- row_grad: float32 [8, 1024, 256], P('dp', 'proto')
- new_student: float32 [256, 131072], P('dp', 'proto')
- new_first: float32 [256, 131072], P('dp', 'proto')
- new_second: float32 [256, 131072], P('dp', 'proto')
- new_teacher: float32 [256, 131072], P('dp', 'proto')
- loss: float32 [], replicated
Inputs may be any that keep to these rules, and one draw needn't show every extreme that they name: `masked_rows`: for each data group and each index of proto in order, 64 distinct positions among that device's 128 patches, ascending; position 0 and position 127 of every device are always masked. `student_proto`: finite entries. `teacher_proto`: finite entries. `first_moment`: finite entries. `second_moment`: positive entries.
All inputs are finite; a program needn't handle non-finite values.
Results may differ from a plain program's by a relative error of at most 0.014.
Values may be sent and summed in bfloat16 or wider, within the bound.
A program may use at most 256 MiB of HBM per device.

v0:
```python
import jax
import jax.numpy as jnp
from jax import lax
from jax.sharding import PartitionSpec as P

PATCH_IMG = 256
student_temp = 0.1
teacher_temp = 0.07
beta_one = 0.9
beta_two = 0.999
fix_one = 0.9999734386011124
fix_two = 0.09520785288629038
learn_rate = 0.002
decay_rate = 0.04
teacher_keep = 0.994


def unit_rows(raw_rows):
    inverse = lax.rsqrt(jnp.sum(raw_rows * raw_rows, axis=-1, keepdims=True) + 1e-06)
    return (raw_rows * inverse, inverse)


def local(
    student_patch,
    teacher_patch,
    patch_image,
    masked_rows,
    student_proto,
    teacher_proto,
    first_moment,
    second_moment,
    centre,
):
    picked = masked_rows[0]
    mask_count = picked.shape[0]
    patch_count = patch_image.shape[1]
    proto_count = lax.axis_size("proto")
    data_count = lax.axis_size("dp")
    raw_student = student_patch[0][picked].astype(jnp.float32)
    raw_teacher = teacher_patch[0][picked].astype(jnp.float32)
    unit_student, inv_student = unit_rows(raw_student)
    unit_teacher, inv_teacher = unit_rows(raw_teacher)
    stacked = jnp.stack([unit_student, unit_teacher]).astype(jnp.bfloat16)
    gathered, image_ids = (
        lax.all_gather(stacked, "proto", axis=1, tiled=True),
        lax.all_gather(patch_image[0][picked], "proto", axis=0, tiled=True),
    )
    rows_student = gathered[0]
    rows_teacher = gathered[1]
    student_w = student_proto.astype(jnp.bfloat16)
    teacher_w = teacher_proto.astype(jnp.bfloat16)
    student_logit = (
        jnp.dot(rows_student, student_w, preferred_element_type=jnp.float32) / student_temp
    )
    teacher_raw = jnp.dot(rows_teacher, teacher_w, preferred_element_type=jnp.float32)
    teacher_logit = (teacher_raw - centre) / teacher_temp
    peak_s, peak_t = lax.pmax(
        (jnp.max(student_logit, axis=1), jnp.max(teacher_logit, axis=1)), "proto"
    )
    exp_s = jnp.exp(student_logit - peak_s[:, None])
    exp_t = jnp.exp(teacher_logit - peak_t[:, None])
    total_s, total_t = lax.psum((jnp.sum(exp_s, axis=1), jnp.sum(exp_t, axis=1)), "proto")
    prob_s = exp_s / total_s[:, None]
    prob_t = exp_t / total_t[:, None]
    labels = jnp.arange(patch_count * proto_count // PATCH_IMG, dtype=jnp.int32)
    matches = (image_ids[:, None] == labels[None, :]).astype(jnp.float32)
    counts = jnp.sum(matches, axis=0)
    per_row = jnp.dot(matches, counts, precision=lax.Precision.HIGHEST)
    row_ratio = mask_count * PATCH_IMG / patch_count
    weights = row_ratio / per_row
    log_total = peak_s + jnp.log(total_s)
    partial_loss = jnp.sum(weights * jnp.sum(prob_t * (log_total[:, None] - student_logit), axis=1))
    grad_logit = (weights[:, None] * (prob_s - prob_t) / student_temp).astype(jnp.bfloat16)
    unit_grad = lax.psum_scatter(
        lax.dot_general(
            grad_logit, student_w, (((1,), (1,)), ((), ())), preferred_element_type=jnp.float32
        ).astype(jnp.bfloat16),
        "proto",
        scatter_dimension=0,
        tiled=True,
    ).astype(jnp.float32)
    row_grad = (
        inv_student * unit_grad
        - inv_student
        * inv_student
        * inv_student
        * raw_student
        * jnp.sum(raw_student * unit_grad, axis=-1, keepdims=True)
    )
    slab_rows = first_moment.shape[0]
    slab_start = lax.axis_index("dp") * slab_rows
    proto_grad = lax.psum_scatter(
        lax.dot_general(
            rows_student, grad_logit, (((0,), (0,)), ((), ())), preferred_element_type=jnp.float32
        ).astype(jnp.bfloat16),
        "dp",
        scatter_dimension=0,
        tiled=True,
    ).astype(jnp.float32)
    loss_sum = lax.psum(partial_loss, ("dp", "proto"))
    rows_total = mask_count * proto_count * data_count
    own_student = lax.dynamic_slice_in_dim(student_proto, slab_start, slab_rows, 0)
    own_teacher = lax.dynamic_slice_in_dim(teacher_proto, slab_start, slab_rows, 0)
    new_first = beta_one * first_moment + (1.0 - beta_one) * proto_grad
    new_second = beta_two * second_moment + (1.0 - beta_two) * proto_grad * proto_grad
    step_size = new_first / fix_one / (jnp.sqrt(new_second / fix_two) + 1e-08)
    new_student = own_student - learn_rate * (step_size + decay_rate * own_student)
    new_teacher = teacher_keep * own_teacher + (1.0 - teacher_keep) * new_student
    loss = loss_sum / rows_total
    return (row_grad[None], new_student, new_first, new_second, new_teacher, loss)


def solution(mesh):
    in_specs = (
        P("dp", "proto", None),
        P("dp", "proto", None),
        P("dp", "proto"),
        P("dp", "proto"),
        P(None, "proto"),
        P(None, "proto"),
        P("dp", "proto"),
        P("dp", "proto"),
        P("proto"),
    )
    out_specs = (
        P("dp", "proto", None),
        P("dp", "proto"),
        P("dp", "proto"),
        P("dp", "proto"),
        P("dp", "proto"),
        P(),
    )
    return jax.shard_map(local, mesh=mesh, in_specs=in_specs, out_specs=out_specs, check_vma=False)
```

profile of v0, /device:TPU:0, one launch (start us, length us, event | category | flops | bytes accessed | tf_op | source)
XLA Modules:
  0.0 364.9 jit_solution(13910082086111725495)
XLA Ops:
  7.2 0.0 copy-start
  7.2 0.0 copy-start.6
  7.2 0.0 all-gather.3.cloned.1.call-start
  7.2 0.7 fusion.27
  7.9 0.1 copy-done
  8.0 0.7 gather_fusion
  8.7 0.1 fusion.20
  8.8 1.5 gather_fusion.2
  10.3 0.1 fusion.19
  10.5 0.1 fusion.18
  10.6 0.6 pad_maximum_fusion
  11.2 0.0 all-gather.3.cloned.1.call-update
  11.2 0.0 reduce-scatter.3.cloned.1.call-start
  11.3 1.4 gather_fusion.1
  12.7 1.2 dynamic-slice
  14.6 0.2 dynamic-update-slice
  14.9 12.9 %all-reduce = s32[1024]{0:T(1024)S(1)} all-reduce(s32[1024]{0:T(1024)S(1)} %dynamic-update-slice), channel_id=2, replica_groups=mesh['dp'=8,'proto'=16] {'proto'}, use_global_device_ids=true, to_apply=%add | all-reduce | flops 1024 | bytes 8192
  27.8 0.1 convert_reduce_fusion
  27.9 0.1 fusion.25
  28.0 18.0 %all-gather.3.cloned.1.call-done = bf16[2,1024,256]{2,1,0:T(8,128)(2,1)} async-done(((bf16[2,64,256]{2,1,0:T(8,128)(2,1)}), bf16[2,1024,256]{2,1,0:T(8,128)(2,1)}) %all-gather.3.cloned.1.call-update) | async-done | bytes 1048592 | tf_op jit(solution)/shard_map/all_gather | solution.py:45
  46.1 0.0 copy-start.3
  46.1 0.0 copy-start.4
  46.1 16.0 %multiply_reduce_fusion.1 = (f32[1024]{0:T(1024)S(1)}, f32[1024,8192]{1,0:T(8,128)}) fusion(f32[256,8192]{1,0:T(8,128)} %param.13, bf16[2,1024,256]{2,1,0:T(8,128)(2,1)} %all-gather.3.cloned.1.call-done), kind=kOutput, calls=%fused_computation.10 | convolution fusion | flops 4313840640 | bytes 42471424 | tf_op jit(solution)/shard_map/dot_general | solution.py:53
  62.0 0.0 copy-done.6
  62.0 0.0 copy-done.3
  62.0 0.0 copy-done.4
  62.0 13.4 %fusion.1 = (f32[1024]{0:T(1024)S(1)}, f32[1024,8192]{1,0:T(8,128)}) fusion(f32[8192]{0:T(1024)S(1)} %copy-done.6, f32[256,8192]{1,0:T(8,128)S(1)} %copy-done.3, bf16[2,1024,256]{2,1,0:T(8,128)(2,1)S(1)} %copy-done.4), kind=kOutput, calls=%fused_computation.9 | convolution fusion | flops 4322229248 | bytes 42504192 | tf_op jit(solution)/shard_map/dot_general | solution.py:55
  75.5 29.6 %all-reduce.2 = (f32[1024]{0:T(1024)S(1)}, f32[1024]{0:T(1024)S(1)}) all-reduce(f32[1024]{0:T(1024)S(1)} %get-tuple-element.18, f32[1024]{0:T(1024)S(1)} %get-tuple-element.20), channel_id=1, replica_groups=mesh['dp'=8,'proto'=16] {'proto'}, use_global_device_ids=true, to_apply=%region_4.0 | all-reduce | flops 2048 | bytes 16384 | tf_op jit(solution)/shard_map/pmax | solution.py:57
  105.0 0.0 copy-start.2
  105.1 15.3 %fusion.3 = f32[1024]{0:T(1024)S(1)} fusion(f32[1024,8192]{1,0:T(8,128)} %get-tuple-element.21, f32[1024]{0:T(1024)S(1)} %get-tuple-element.9, f32[8192]{0:T(1024)S(1)} %copy-done.6), kind=kLoop, calls=%fused_computation.12 | loop fusion | flops 33553408 | bytes 33595392 | tf_op jit(solution)/shard_map/reduce_sum | solution.py:62
  120.4 4.8 %copy-done.2 = f32[1024,8192]{1,0:T(8,128)S(1)} copy-done((f32[1024,8192]{1,0:T(8,128)S(1)}, f32[1024,8192]{1,0:T(8,128)}, u32[]{:S(2)}) %copy-start.2) | copy-done | bytes 33554456
  125.2 6.7 %fusion = f32[1024]{0:T(1024)S(1)} fusion(f32[1024,8192]{1,0:T(8,128)S(1)} %copy-done.2, f32[1024]{0:T(1024)S(1)} %get-tuple-element.8), kind=kLoop, calls=%fused_computation.8 | loop fusion | flops 25164800 | bytes 33562624 | tf_op jit(solution)/shard_map/reduce_sum | solution.py:62
  131.9 27.8 %all-reduce.1 = (f32[1024]{0:T(1024)S(1)}, f32[1024]{0:T(1024)S(1)}) all-reduce(f32[1024]{0:T(1024)S(1)} %fusion, f32[1024]{0:T(1024)S(1)} %fusion.3), channel_id=1, replica_groups=mesh['dp'=8,'proto'=16] {'proto'}, use_global_device_ids=true, to_apply=%region_6.0 | all-reduce | flops 2048 | bytes 16384 | tf_op jit(solution)/shard_map/psum | solution.py:62
  159.7 0.0 copy-start.1
  159.7 31.3 %multiply_reduce_fusion = (f32[1024]{0:T(1024)S(1)}, bf16[1024,8192]{1,0:T(8,128)(2,1)}) fusion(f32[1024,8192]{1,0:T(8,128)} %get-tuple-element.19, f32[1024]{0:T(1024)S(1)} %log_add_fusion, f32[1024]{0:T(1024)S(1)} %get-tuple-element.7, f32[1024]{0:T(1024)S(1)} %get-tuple-element.9, f32[1024,8192]{1,0:T(8,128)} %get-tuple-element.21, f32[8192]{0:T(1024)S(1)} %copy-done.6, ...), kind=kLoop, calls=%fused_computation.3 | loop fusion | flops 117439488 | bytes 83947520 | tf_op jit(solution)/shard_map/reduce_sum | solution.py:72
  191.0 0.0 copy-start.5
  191.0 13.6 %fusion.10 = bf16[1024,256]{1,0:T(8,128)(2,1)} fusion(bf16[1024,8192]{1,0:T(8,128)(2,1)} %get-tuple-element.15, f32[256,8192]{1,0:T(8,128)} %param.13), kind=kOutput, calls=%fused_computation.22 | convolution fusion | flops 4297326592 | bytes 25690112 | tf_op jit(solution)/shard_map/dot_general | solution.py:75
  204.6 0.0 reduce-scatter.3.cloned.1.call-update
  204.6 0.0 reduce-scatter.5.cloned.1.call-start
  204.7 12.1 %convolution_convert_fusion = bf16[256,8192]{1,0:T(8,128)(2,1)} fusion(bf16[1024,8192]{1,0:T(8,128)(2,1)} %get-tuple-element.15, bf16[2,1024,256]{2,1,0:T(8,128)(2,1)S(1)} %copy-done.4), kind=kOutput, calls=%fused_computation.13 | convolution fusion | flops 4297064448 | bytes 21495808 | tf_op jit(solution)/shard_map/dot_general | solution.py:93
  216.7 0.0 reduce-scatter.5.cloned.1.call-update
  216.7 0.6 multiply_reduce_fusion.2
  217.4 66.2 %psum.23 = f32[]{:T(128)} all-reduce(f32[]{:T(128)} %multiply_reduce_fusion.2), channel_id=1, replica_groups=mesh['dp'=8,'proto'=16] {'dp','proto'}, use_global_device_ids=true, to_apply=%region_16.0 | all-reduce | flops 1 | bytes 8 | tf_op jit(solution)/shard_map/psum | solution.py:100
  284.2 0.0 reduce-scatter.3.cloned.1.call-done
  284.3 0.9 fusion.22
  285.1 1.5 fusion.16
  286.6 66.0 %reduce-scatter.5.cloned.1.call-done = bf16[32,8192]{1,0:T(8,128)(2,1)} async-done(((bf16[256,8192]{1,0:T(8,128)(2,1)}), bf16[32,8192]{1,0:T(8,128)(2,1)}) %reduce-scatter.5.cloned.1.call-update) | async-done | bytes 524304 | tf_op jit(solution)/shard_map/reduce_scatter | solution.py:92
  352.6 0.0 copy-done.5
  352.6 4.7 %multiply_add_fusion = (f32[32,8192]{1,0:T(8,128)}, f32[32,8192]{1,0:T(8,128)}, f32[32,8192]{1,0:T(8,128)}, f32[32,8192]{1,0:T(8,128)}) fusion(f32[256,8192]{1,0:T(8,128)} %param.14, s32[]{:T(128)S(6)} %select_n.17, f32[256,8192]{1,0:T(8,128)} %param.13, bf16[32,8192]{1,0:T(8,128)(2,1)} %reduce-scatter.5.cloned.1.call-done, f32[32,8192]{1,0:T(8,128)S(1)} %copy-done.5, ...), kind=kLoop, calls=%fused_computation.25 | loop fusion | flops 4980736 | bytes 8912900 | tf_op jit(solution)/shard_map/add | solution.py:108
  357.3 0.0 copy-done.1
  (6 shorter events, 0.0 us)
Async XLA Ops:
  7.2 0.8 copy-start
  7.2 54.9 %copy-start.6 = (f32[8192]{0:T(1024)S(1)}, f32[8192]{0:T(1024)}, u32[]{:S(2)}) copy-start(f32[8192]{0:T(1024)} %param.17) | copy-start | bytes 98308
  7.2 38.9 %all-gather.3.cloned.1.call-start = ((), (), s32[]{:S(2)}) async-start(), calls=%async_computation.2 | async-start | bytes 1114112 | tf_op jit(solution)/shard_map/all_gather | solution.py:45
  11.2 273.0 %reduce-scatter.3.cloned.1.call-start = ((), (), s32[]{:S(2)}) async-start(), calls=%async_computation.3 | async-start | bytes 557056 | tf_op jit(solution)/shard_map/reduce_scatter | solution.py:74
  46.1 16.0 %copy-start.3 = (f32[256,8192]{1,0:T(8,128)S(1)}, f32[256,8192]{1,0:T(8,128)}, u32[]{:S(2)}) copy-start(f32[256,8192]{1,0:T(8,128)} %param.14) | copy-start | bytes 25165828
  46.1 16.0 %copy-start.4 = (bf16[2,1024,256]{2,1,0:T(8,128)(2,1)S(1)}, bf16[2,1024,256]{2,1,0:T(8,128)(2,1)}, u32[]{:S(2)}) copy-start(bf16[2,1024,256]{2,1,0:T(8,128)(2,1)} %all-gather.3.cloned.1.call-done) | copy-start | bytes 3145732
  105.0 20.2 %copy-start.2 = (f32[1024,8192]{1,0:T(8,128)S(1)}, f32[1024,8192]{1,0:T(8,128)}, u32[]{:S(2)}) copy-start(f32[1024,8192]{1,0:T(8,128)} %get-tuple-element.19) | copy-start | bytes 100663296
  159.7 197.6 %copy-start.1 = (bf16[1,128,256]{2,1,0:T(8,128)(2,1)S(1)}, bf16[1,128,256]{2,1,0:T(8,128)(2,1)}, u32[]{:S(2)}) copy-start(bf16[1,128,256]{2,1,0:T(8,128)(2,1)} %param.9) | copy-start | bytes 196612
  191.0 161.6 %copy-start.5 = (f32[32,8192]{1,0:T(8,128)S(1)}, f32[32,8192]{1,0:T(8,128)}, u32[]{:S(2)}) copy-start(f32[32,8192]{1,0:T(8,128)} %param.15) | copy-start | bytes 3145732
  204.6 148.0 %reduce-scatter.5.cloned.1.call-start = ((), (), s32[]{:S(2)}) async-start(), calls=%async_computation.4 | async-start | bytes 4718592 | tf_op jit(solution)/shard_map/reduce_scatter | solution.py:92
Sparse Core Ops, SparseCore 0:
  11.4 34.6 all-gather.2
  204.7 60.0 reduce-scatter.2
  268.7 83.8 reduce-scatter.4
where the time goes:
time: 365 us
  blocking collectives  136 us (37%)
  waiting for transfers between devices  84 us (23%)
  other arithmetic  62.7 us (17%)
  matrix products  55.2 us (15%)
  between operations  16.3 us (4%)
  local copies, waits for them, and re-layouts  10.1 us (3%)
    psum x1, blocking collectives, local(): loss_sum = lax.psum(partial_loss, ('dp', 'proto'))  66.2 us
    reduce_scatter x1, waiting for transfers between devices, local(): lax.psum_scatter(lax.dot_general(rows_student, grad_logit, (((0,), (0,)),...  66 us
    reduce_sum x1, other arithmetic, local(): jnp.sum(prob_t * (log_total[:, None] - student_logit), axis=1)  31.3 us
    pmax x1, blocking collectives, local(): lax.pmax((jnp.max(student_logit, axis=1), jnp.max(teacher_logit, axis=1))...  29.6 us
    psum x1, blocking collectives, local(): lax.psum((jnp.sum(exp_s, axis=1), jnp.sum(exp_t, axis=1)), 'proto')  27.8 us
    all_gather x1, waiting for transfers between devices, local(): lax.all_gather(stacked, 'proto', axis=1, tiled=True)  18 us
    dot_general x1, matrix products, local(): jnp.dot(rows_student, student_w, preferred_element_type=jnp.float32)  16 us
    reduce_sum x1, other arithmetic, local(): jnp.sum(exp_t, axis=1)  15.3 us
  transfers between devices with their start and end apart: 3, of which 2 were waited for; matrix products, arithmetic and copies ran while one was open for 5% of the time, Pallas kernels for 0%

commit v1 on v0

--- a/solution.py
+++ b/solution.py
@@ -13,6 +13,11 @@
 learn_rate = 0.002
 decay_rate = 0.04
 teacher_keep = 0.994
+
+
+def gather_over(x, mesh_axis, dim):
+    sent = jnp.stack([x] * lax.axis_size(mesh_axis))
+    return jnp.concatenate(lax.all_to_all(sent, mesh_axis, 0, 0), axis=dim)
 
 
 def unit_rows(raw_rows):
@@ -42,7 +47,7 @@
     unit_teacher, inv_teacher = unit_rows(raw_teacher)
     stacked = jnp.stack([unit_student, unit_teacher]).astype(jnp.bfloat16)
     gathered, image_ids = (
-        lax.all_gather(stacked, "proto", axis=1, tiled=True),
+        gather_over(stacked, "proto", 1),
         lax.all_gather(patch_image[0][picked], "proto", axis=0, tiled=True),
     )
     rows_student = gathered[0]

time: 365 us -> 362 us (level)
  waiting for transfers between devices: 84 us -> 66.8 us
  other arithmetic: 62.7 us -> 68.8 us
  starting transfers between devices: 0.12 us -> 5.95 us
  blocking collectives: 136 us -> 140 us
    all_gather x1 -> x0, waiting for transfers between devices: 18 us -> none  [local(): lax.all_gather(stacked, 'proto', axis=1, tiled=True)]
    reduce_sum x1, other arithmetic: 6.66 us -> 14.1 us  [local(): jnp.sum(exp_s, axis=1)]
    all_to_all x0 -> x1, starting transfers between devices: none -> 5.87 us  [gather_over(): return jnp.concatenate(lax.all_to_all(sent, mesh_axis, 0, 0), axis=dim)]
    unnamed x1, blocking collectives: 12.9 us -> 18.1 us
    unnamed x17 -> x15, local copies, waits for them, and re-layouts: 6.44 us -> 1.66 us
  transfers between devices with their start and end apart: 3 -> 3, of which waited for: 2 -> 1; matrix products, arithmetic and copies ran while one was open for 5% -> 5% of each run, Pallas kernels for 0% -> 0%
where the time goes in v1:
time: 362 us; the launch traced here: 361 us
  blocking collectives  140 us (39%)
  other arithmetic  68.8 us (19%)
  waiting for transfers between devices  66.8 us (18%)
  matrix products  55.9 us (15%)
  between operations  16.7 us (5%)
  local copies, waits for them, and re-layouts  6.45 us (2%)
  starting transfers between devices  5.95 us (2%)
    reduce_scatter x1, waiting for transfers between devices, local(): lax.psum_scatter(lax.dot_general(rows_student, grad_logit, (((0,), (0,)),...  66.8 us
    psum x1, blocking collectives, local(): loss_sum = lax.psum(partial_loss, ('dp', 'proto'))  66.6 us
    reduce_sum x1, other arithmetic, local(): jnp.sum(prob_t * (log_total[:, None] - student_logit), axis=1)  31.3 us
    psum x1, blocking collectives, local(): lax.psum((jnp.sum(exp_s, axis=1), jnp.sum(exp_t, axis=1)), 'proto')  27.8 us
    pmax x1, blocking collectives, local(): lax.pmax((jnp.max(student_logit, axis=1), jnp.max(teacher_logit, axis=1))...  27.6 us
    unnamed x1, blocking collectives  18.1 us
    dot_general x1, matrix products, local(): jnp.dot(rows_student, student_w, preferred_element_type=jnp.float32)  16.7 us
    reduce_sum x1, other arithmetic, local(): jnp.sum(exp_t, axis=1)  14.7 us
  transfers between devices with their start and end apart: 3, of which 1 were waited for; matrix products, arithmetic and copies ran while one was open for 5% of the time, Pallas kernels for 0%

profile of v1, /device:TPU:0, one launch (start us, length us, event | category | flops | bytes accessed | tf_op | source)
XLA Modules:
  0.0 360.7 jit_solution(7419126667572867382)
XLA Ops:
  7.2 0.0 copy-start
  7.2 0.0 copy-start.3
  7.2 0.7 fusion.27
  7.9 0.1 copy-done
  8.0 0.7 gather_fusion
  8.7 0.1 fusion.20
  8.8 1.5 gather_fusion.2
  10.3 0.1 fusion.19
  10.5 0.1 fusion.18
  10.6 1.1 stack.5
  11.7 5.9 %all-to-all-start = ((bf16[16,2,64,256]{3,2,1,0:T(8,128)(2,1)}), bf16[16,2,64,256]{3,2,1,0:T(8,128)(2,1)S(1)}, u32[]{:S(2)}, u32[]{:S(2)}) async-start(bf16[16,2,64,256]{3,2,1,0:T(8,128)(2,1)} %stack.5), calls=%async_computation | async-start | bytes 2097152 | tf_op jit(solution)/shard_map/all_to_all | solution.py:20
  17.6 0.0 reduce-scatter.3.cloned.1.call-start
  17.6 1.4 gather_fusion.1
  19.0 1.2 dynamic-slice
  21.0 0.2 dynamic-update-slice
  21.2 18.1 %all-reduce = s32[1024]{0:T(1024)S(1)} all-reduce(s32[1024]{0:T(1024)S(1)} %dynamic-update-slice), channel_id=2, replica_groups=mesh['dp'=8,'proto'=16] {'proto'}, use_global_device_ids=true, to_apply=%add | all-reduce | flops 1024 | bytes 8192
  39.3 0.1 convert_reduce_fusion
  39.4 0.1 fusion.25
  39.6 0.0 all-to-all-done
  39.6 0.0 slice-start
  39.6 0.1 fusion.31
  39.7 0.0 slice-start.1
  39.7 16.7 %multiply_reduce_fusion.1 = (f32[1024]{0:T(1024)S(1)}, f32[1024,8192]{1,0:T(8,128)}) fusion(bf16[1024,256]{1,0:T(8,128)(2,1)S(1)} %bitcast.38, f32[256,8192]{1,0:T(8,128)} %param.13), kind=kOutput, calls=%fused_computation.10 | convolution fusion | flops 4313840640 | bytes 42471424 | tf_op jit(solution)/shard_map/dot_general | solution.py:58
  56.4 0.0 copy-done.3
  56.4 0.0 slice-done
  56.4 0.0 slice-done.1
  56.4 13.4 %fusion.1 = (f32[1024]{0:T(1024)S(1)}, f32[1024,8192]{1,0:T(8,128)}) fusion(f32[8192]{0:T(1024)S(1)} %copy-done.3, bf16[1024,256]{1,0:T(8,128)(2,1)S(1)} %bitcast.41, f32[256,8192]{1,0:T(8,128)S(1)} %bitcast.37), kind=kOutput, calls=%fused_computation.9 | convolution fusion | flops 4322229248 | bytes 42504192 | tf_op jit(solution)/shard_map/dot_general | solution.py:60
  69.9 27.6 %all-reduce.2 = (f32[1024]{0:T(1024)S(1)}, f32[1024]{0:T(1024)S(1)}) all-reduce(f32[1024]{0:T(1024)S(1)} %get-tuple-element.20, f32[1024]{0:T(1024)S(1)} %get-tuple-element.22), channel_id=1, replica_groups=mesh['dp'=8,'proto'=16] {'proto'}, use_global_device_ids=true, to_apply=%region_4.0 | all-reduce | flops 2048 | bytes 16384 | tf_op jit(solution)/shard_map/pmax | solution.py:62
  97.5 14.7 %fusion.3 = f32[1024]{0:T(1024)S(1)} fusion(f32[1024,8192]{1,0:T(8,128)} %get-tuple-element.23, f32[1024]{0:T(1024)S(1)} %get-tuple-element.9, f32[8192]{0:T(1024)S(1)} %copy-done.3), kind=kLoop, calls=%fused_computation.12 | loop fusion | flops 33553408 | bytes 33595392 | tf_op jit(solution)/shard_map/reduce_sum | solution.py:67
  112.2 14.1 %fusion = f32[1024]{0:T(1024)S(1)} fusion(f32[1024,8192]{1,0:T(8,128)} %get-tuple-element.21, f32[1024]{0:T(1024)S(1)} %get-tuple-element.8), kind=kLoop, calls=%fused_computation.8 | loop fusion | flops 25164800 | bytes 33562624 | tf_op jit(solution)/shard_map/reduce_sum | solution.py:67
  126.2 27.8 %all-reduce.1 = (f32[1024]{0:T(1024)S(1)}, f32[1024]{0:T(1024)S(1)}) all-reduce(f32[1024]{0:T(1024)S(1)} %fusion, f32[1024]{0:T(1024)S(1)} %fusion.3), channel_id=1, replica_groups=mesh['dp'=8,'proto'=16] {'proto'}, use_global_device_ids=true, to_apply=%region_6.0 | all-reduce | flops 2048 | bytes 16384 | tf_op jit(solution)/shard_map/psum | solution.py:67
  154.1 0.0 copy-start.1
  154.1 31.3 %multiply_reduce_fusion = (f32[1024]{0:T(1024)S(1)}, bf16[1024,8192]{1,0:T(8,128)(2,1)}) fusion(f32[1024,8192]{1,0:T(8,128)} %get-tuple-element.21, f32[1024]{0:T(1024)S(1)} %log_add_fusion, f32[1024]{0:T(1024)S(1)} %get-tuple-element.7, f32[1024]{0:T(1024)S(1)} %get-tuple-element.9, f32[1024,8192]{1,0:T(8,128)} %get-tuple-element.23, f32[8192]{0:T(1024)S(1)} %copy-done.3, ...), kind=kLoop, calls=%fused_computation.3 | loop fusion | flops 117439488 | bytes 83947520 | tf_op jit(solution)/shard_map/reduce_sum | solution.py:77
  185.4 0.0 copy-start.2
  185.4 13.6 %fusion.10 = bf16[1024,256]{1,0:T(8,128)(2,1)} fusion(bf16[1024,8192]{1,0:T(8,128)(2,1)} %get-tuple-element.15, f32[256,8192]{1,0:T(8,128)} %param.13), kind=kOutput, calls=%fused_computation.22 | convolution fusion | flops 4297326592 | bytes 25690112 | tf_op jit(solution)/shard_map/dot_general | solution.py:80
  198.9 0.0 reduce-scatter.3.cloned.1.call-update
  199.0 0.0 reduce-scatter.5.cloned.1.call-start
  199.0 12.1 %convolution_convert_fusion = bf16[256,8192]{1,0:T(8,128)(2,1)} fusion(bf16[1024,256]{1,0:T(8,128)(2,1)S(1)} %bitcast.39, bf16[1024,8192]{1,0:T(8,128)(2,1)} %get-tuple-element.15), kind=kOutput, calls=%fused_computation.13 | convolution fusion | flops 4297064448 | bytes 21495808 | tf_op jit(solution)/shard_map/dot_general | solution.py:98
  211.1 0.0 reduce-scatter.5.cloned.1.call-update
  211.1 0.6 multiply_reduce_fusion.2
  211.7 66.6 %psum.23 = f32[]{:T(128)} all-reduce(f32[]{:T(128)} %multiply_reduce_fusion.2), channel_id=1, replica_groups=mesh['dp'=8,'proto'=16] {'dp','proto'}, use_global_device_ids=true, to_apply=%region_16.0 | all-reduce | flops 1 | bytes 8 | tf_op jit(solution)/shard_map/psum | solution.py:105
  279.0 0.0 reduce-scatter.3.cloned.1.call-done
  279.0 0.9 fusion.22
  279.9 1.5 fusion.16
  281.3 66.8 %reduce-scatter.5.cloned.1.call-done = bf16[32,8192]{1,0:T(8,128)(2,1)} async-done(((bf16[256,8192]{1,0:T(8,128)(2,1)}), bf16[32,8192]{1,0:T(8,128)(2,1)}) %reduce-scatter.5.cloned.1.call-update) | async-done | bytes 524304 | tf_op jit(solution)/shard_map/reduce_scatter | solution.py:97
  348.1 0.0 copy-done.2
  348.1 4.6 %multiply_add_fusion = (f32[32,8192]{1,0:T(8,128)}, f32[32,8192]{1,0:T(8,128)}, f32[32,8192]{1,0:T(8,128)}, f32[32,8192]{1,0:T(8,128)}) fusion(f32[256,8192]{1,0:T(8,128)} %param.14, s32[]{:T(128)S(6)} %select_n.17, f32[256,8192]{1,0:T(8,128)} %param.13, bf16[32,8192]{1,0:T(8,128)(2,1)} %reduce-scatter.5.cloned.1.call-done, f32[32,8192]{1,0:T(8,128)S(1)} %copy-done.2, ...), kind=kLoop, calls=%fused_computation.25 | loop fusion | flops 4980736 | bytes 8912900 | tf_op jit(solution)/shard_map/add | solution.py:113
  352.8 0.0 copy-done.1
  (8 shorter events, 0.0 us)
Async XLA Ops:
  7.2 0.8 copy-start
  7.2 49.2 %copy-start.3 = (f32[8192]{0:T(1024)S(1)}, f32[8192]{0:T(1024)}, u32[]{:S(2)}) copy-start(f32[8192]{0:T(1024)} %param.17) | copy-start | bytes 98308
  11.7 27.9 %all-to-all-start = ((bf16[16,2,64,256]{3,2,1,0:T(8,128)(2,1)}), bf16[16,2,64,256]{3,2,1,0:T(8,128)(2,1)S(1)}, u32[]{:S(2)}, u32[]{:S(2)}) async-start(bf16[16,2,64,256]{3,2,1,0:T(8,128)(2,1)} %stack.5), calls=%async_computation | async-start | bytes 2097152 | tf_op jit(solution)/shard_map/all_to_all | solution.py:20
  17.6 261.4 %reduce-scatter.3.cloned.1.call-start = ((), (), s32[]{:S(2)}) async-start(), calls=%async_computation.3 | async-start | bytes 557056 | tf_op jit(solution)/shard_map/reduce_scatter | solution.py:79
  39.6 16.8 %slice-start = ((s8[8388608]{0:T(1024)(128)(4,1)}), s8[4194304]{0:T(1024)(128)(4,1)S(1)}, s32[]{:S(2)}) async-start(s8[8388608]{0:T(1024)(128)(4,1)} %bitcast.36), calls=%async_computation.5 | async-start | bytes 8388608
  39.7 16.7 %slice-start.1 = ((s8[8388608]{0:T(1024)(128)(4,1)}), s8[4194304]{0:T(1024)(128)(4,1)S(1)}, s32[]{:S(2)}) async-start(s8[8388608]{0:T(1024)(128)(4,1)} %bitcast.36), calls=%async_computation.6 | async-start | bytes 8388608
  154.1 198.7 %copy-start.1 = (bf16[1,128,256]{2,1,0:T(8,128)(2,1)S(1)}, bf16[1,128,256]{2,1,0:T(8,128)(2,1)}, u32[]{:S(2)}) copy-start(bf16[1,128,256]{2,1,0:T(8,128)(2,1)} %param.9) | copy-start | bytes 196612
  185.4 162.8 %copy-start.2 = (f32[32,8192]{1,0:T(8,128)S(1)}, f32[32,8192]{1,0:T(8,128)}, u32[]{:S(2)}) copy-start(f32[32,8192]{1,0:T(8,128)} %param.15) | copy-start | bytes 3145732
  199.0 149.2 %reduce-scatter.5.cloned.1.call-start = ((), (), s32[]{:S(2)}) async-start(), calls=%async_computation.4 | async-start | bytes 4718592 | tf_op jit(solution)/shard_map/reduce_scatter | solution.py:97
Sparse Core Ops, SparseCore 0:
  199.1 61.0 reduce-scatter.2
  264.0 84.0 reduce-scatter.4
